TPU v7x, 32 devices: a whole 2x2x4 slice. The times are simulated.
32 devices in a mesh: dp: 4 (over x, core), ctx: 2 (over y), tensor: 4 (over z).
Axes of the slice: x: 2, y: 2, z: 4, core: 2. Of those that a mesh axis runs over, the one named last changes fastest.
Arguments:
- inputs: bfloat16 [2048, 2048], P(('dp', 'ctx'), 'tensor'), may hold values from -6 to 6
- cotangent: bfloat16 [2048, 2048], P(('dp', 'ctx')), may hold values from -6 to 6
- segments: int32 [4, 512], P('dp'), may hold values from 0 to 15, as said below
- positions: int32 [4, 512], P('dp', 'ctx'), may hold values from 0 to 511, as said below
- attention_gain: bfloat16 [2048], replicated, may hold values from 0.5 to 1.5
- query_weight: bfloat16 [2048, 2048], P(None, 'tensor'), may hold values from -0.125 to 0.125
- key_weight: bfloat16 [2048, 1024], P(None, 'tensor'), may hold values from -0.125 to 0.125
- value_weight: bfloat16 [2048, 1024], P(None, 'tensor'), may hold values from -0.125 to 0.125
- query_gain: bfloat16 [128], replicated, may hold values from 0.5 to 1.5
- key_gain: bfloat16 [128], replicated, may hold values from 0.5 to 1.5
- output_weight: bfloat16 [2048, 2048], P('tensor'), may hold values from -0.75 to 0.75
- feed_gain: bfloat16 [2048], replicated, may hold values from 0.3 to 5, as said below
- gate_weight: bfloat16 [2048, 6144], P(None, 'tensor'), may hold values from -0.125 to 0.125
- up_weight: bfloat16 [2048, 6144], P(None, 'tensor'), may hold values from -0.125 to 0.125
- down_weight: bfloat16 [6144, 2048], P('tensor'), may hold values from -0.078125 to 0.078125
Outputs:
- outputs: bfloat16 [2048, 2048], P(('dp', 'ctx'), 'tensor')
- grad_inputs: float32 [2048, 2048], P(('dp', 'ctx'), 'tensor')
- grad_attention_gain: float32 [2048], P('tensor')
- grad_query_weight: float32 [2048, 2048], P(None, 'tensor')
- grad_key_weight: float32 [2048, 1024], P(None, 'tensor')
- grad_value_weight: float32 [2048, 1024], P(None, 'tensor')
- grad_query_gain: float32 [128], replicated
- grad_key_gain: float32 [128], replicated
- grad_output_weight: float32 [2048, 2048], P('tensor')
- grad_feed_gain: float32 [2048], P('tensor')
- grad_gate_weight: float32 [2048, 6144], P(None, 'tensor')
- grad_up_weight: float32 [2048, 6144], P(None, 'tensor')
- grad_down_weight: float32 [6144, 2048], P('tensor')
Inputs may be any that keep to these rules, and one draw needn't show every extreme that they name: `segments`: in each sequence the document numbers start at 0, never fall, and each document is one run of equal numbers; a sequence holds at most 16 documents. `positions`: a token's position counts from 0 at the first token of its document. `feed_gain`: positive gains.
All inputs are finite; a program needn't handle non-finite values.
Results may differ from a plain program's by a relative error of at most 0.024.
Values may be sent and summed in bfloat16 or wider, within the bound.
No kernel may reach another device: no remote copies, remote signals or barrier semaphores. Data moves between devices by JAX's collectives and lax.ppermute only.
A program may use at most 256 MiB of HBM per device.

v0:
```python
import jax
import jax.numpy as jnp
from jax import lax
from jax.sharding import PartitionSpec as P

HD = 128
EPS = 1e-06
THETA = 1000000.0
NEG = -1e30


def rope_tables(position_row):
    half = HD // 2
    freqs = jnp.exp(-(2.0 * jnp.arange(half, dtype=jnp.float32) / HD) * jnp.log(jnp.float32(THETA)))
    angles = position_row.astype(jnp.float32)[:, None] * freqs[None, :]
    return (jnp.cos(angles)[:, None, :], jnp.sin(angles)[:, None, :])


def rotate(value, cosine, sine):
    half = value.shape[-1] // 2
    first = value[..., :half]
    second = value[..., half:]
    return jnp.concatenate(
        [first * cosine - second * sine, second * cosine + first * sine], axis=-1
    )


def head_prepare(raw, gain, cosine, sine):
    count = raw.shape[0]
    heads = raw.reshape(count, -1, HD)
    normed = heads * lax.rsqrt(jnp.mean(heads * heads, axis=-1, keepdims=True) + EPS) * gain
    return rotate(normed, cosine, sine).reshape(count, -1)


def matmul(left, right):
    return jnp.dot(left, right, preferred_element_type=jnp.float32)


def per_device(
    inputs,
    cotangent,
    segments,
    positions,
    attention_gain,
    query_weight,
    key_weight,
    value_weight,
    query_gain,
    key_gain,
    output_weight,
    feed_gain,
    gate_weight,
    up_weight,
    down_weight,
):
    count = inputs.shape[0]
    shard = inputs.shape[1]
    width = cotangent.shape[1]
    column = lax.axis_index("tensor") * shard
    place = lax.axis_index("ctx")
    kv_local = key_weight.shape[1] // HD
    group = query_weight.shape[1] // key_weight.shape[1]
    factor = HD ** (-0.5)
    block = min(512, count)
    blocks = count // block
    gain_one = attention_gain.astype(jnp.float32)
    gain_two = feed_gain.astype(jnp.float32)
    gain_one_part = lax.dynamic_slice_in_dim(gain_one, column, shard)
    gain_two_part = lax.dynamic_slice_in_dim(gain_two, column, shard)
    cosine, sine = rope_tables(positions[0])
    gathered = lax.all_gather(inputs, "tensor", axis=1, tiled=True).astype(jnp.float32)
    inverse_one = lax.rsqrt(jnp.mean(gathered * gathered, axis=-1, keepdims=True) + EPS)
    unit_one = gathered * inverse_one
    normed_one = (unit_one * gain_one).astype(jnp.bfloat16)
    query_raw = matmul(normed_one, query_weight)
    key_raw = matmul(normed_one, key_weight)
    value_rows = matmul(normed_one, value_weight).astype(jnp.bfloat16)
    query_float, query_pull = jax.vjp(
        lambda raw, gain: head_prepare(raw, gain, cosine, sine),
        query_raw,
        query_gain.astype(jnp.float32),
    )
    key_float, key_pull = jax.vjp(
        lambda raw, gain: head_prepare(raw, gain, cosine, sine),
        key_raw,
        key_gain.astype(jnp.float32),
    )
    query_rows = query_float.astype(jnp.bfloat16)
    key_rows = key_float.astype(jnp.bfloat16)
    segment_row = segments[0]
    all_keys, all_values = (
        lax.all_gather(key_rows, "ctx", axis=0, tiled=True),
        lax.all_gather(value_rows, "ctx", axis=0, tiled=True),
    )
    total_keys = all_keys.shape[0]
    key_index = jnp.arange(total_keys, dtype=jnp.int32)
    row_offset = place * count
    key_heads = all_keys.reshape(total_keys, kv_local, HD)
    value_heads = all_values.reshape(total_keys, kv_local, HD)
    query_blocks = query_rows.reshape(blocks, block, kv_local, group, HD)

    def allowed_mask(index):
        start = index * block
        row_index = row_offset + start + jnp.arange(block, dtype=jnp.int32)
        row_segment = lax.dynamic_slice_in_dim(segment_row, row_offset + start, block)
        return (row_segment[:, None] == segment_row[None, :]) & (
            key_index[None, :] <= row_index[:, None]
        )

    def block_scores(rows, index):
        scores = (
            jnp.einsum("qhgd,khd->hgqk", rows, key_heads, preferred_element_type=jnp.float32)
            * factor
        )
        return jnp.where(allowed_mask(index)[None, None], scores, NEG)

    def forward_block(index):
        rows = query_blocks[index]
        scores = block_scores(rows, index)
        top = jnp.max(scores, axis=-1, keepdims=True)
        raised = jnp.exp(scores - top)
        total = jnp.sum(raised, axis=-1, keepdims=True)
        weights = (raised / total).astype(jnp.bfloat16)
        mixed = jnp.einsum(
            "hgqk,khd->qhgd", weights, value_heads, preferred_element_type=jnp.float32
        )
        return (mixed.astype(jnp.bfloat16), top + jnp.log(total))

    mixed_blocks, log_totals = lax.map(forward_block, jnp.arange(blocks, dtype=jnp.int32))
    mixed_rows = mixed_blocks.reshape(count, -1)
    attention_terms = matmul(mixed_rows, output_weight)
    branch = lax.psum_scatter(attention_terms, "tensor", scatter_dimension=1, tiled=True)
    resid_part = (inputs.astype(jnp.float32) + branch).astype(jnp.bfloat16)
    resid_rows = lax.all_gather(resid_part, "tensor", axis=1, tiled=True).astype(jnp.float32)
    inverse_two = lax.rsqrt(jnp.mean(resid_rows * resid_rows, axis=-1, keepdims=True) + EPS)
    unit_two = resid_rows * inverse_two
    normed_two = (unit_two * gain_two).astype(jnp.bfloat16)
    gate = matmul(normed_two, gate_weight)
    up_rows = matmul(normed_two, up_weight)
    sigmoid = jax.nn.sigmoid(gate)
    silu = gate * sigmoid
    hidden = (silu * up_rows).astype(jnp.bfloat16)
    feed = lax.psum_scatter(
        matmul(hidden, down_weight).astype(jnp.bfloat16), "tensor", scatter_dimension=1, tiled=True
    ).astype(jnp.float32)
    outputs = (resid_part.astype(jnp.float32) + feed).astype(jnp.bfloat16)
    grad_down = matmul(hidden.T, cotangent)
    grad_hidden = matmul(cotangent, down_weight.T)
    grad_gate = (grad_hidden * up_rows * sigmoid * (1.0 + gate * (1.0 - sigmoid))).astype(
        jnp.bfloat16
    )
    grad_up = (grad_hidden * silu).astype(jnp.bfloat16)
    grad_gate_w = matmul(normed_two.T, grad_gate)
    grad_up_w = matmul(normed_two.T, grad_up)
    grad_normed_two = matmul(grad_gate, gate_weight.T) + matmul(grad_up, up_weight.T)
    unit_two_part = lax.dynamic_slice_in_dim(unit_two, column, shard, 1)
    grad_out_part = lax.dynamic_slice_in_dim(cotangent, column, shard, 1).astype(jnp.float32)
    grad_two_part = lax.psum_scatter(grad_normed_two, "tensor", scatter_dimension=1, tiled=True)
    row_term_two = jnp.sum(gain_two_part * grad_two_part * unit_two_part, axis=-1)
    row_total_two = lax.psum(row_term_two, "tensor")
    grad_feed_gain = jnp.sum(grad_two_part * unit_two_part, axis=0)
    grad_resid = (
        grad_out_part
        + inverse_two * (gain_two_part * grad_two_part)
        - unit_two_part * (inverse_two / width) * row_total_two[:, None]
    )
    grad_resid_rows = lax.all_gather(grad_resid.astype(jnp.bfloat16), "tensor", axis=1, tiled=True)
    grad_output_w = matmul(mixed_rows.T, grad_resid_rows)
    grad_mixed = matmul(grad_resid_rows, output_weight.T).astype(jnp.bfloat16)
    grad_mixed_blocks = grad_mixed.reshape(blocks, block, kv_local, group, HD)

    def backward_block(carry, index):
        key_total, value_total = carry
        rows = query_blocks[index]
        grad_rows = grad_mixed_blocks[index]
        scores = block_scores(rows, index)
        probs = jnp.exp(scores - log_totals[index])
        grad_probs = jnp.einsum(
            "qhgd,khd->hgqk", grad_rows, value_heads, preferred_element_type=jnp.float32
        )
        delta = jnp.sum(probs * grad_probs, axis=-1, keepdims=True)
        grad_scores = (probs * (grad_probs - delta)).astype(jnp.bfloat16)
        grad_query = (
            jnp.einsum("hgqk,khd->qhgd", grad_scores, key_heads, preferred_element_type=jnp.float32)
            * factor
        )
        key_total = (
            key_total
            + jnp.einsum("hgqk,qhgd->khd", grad_scores, rows, preferred_element_type=jnp.float32)
            * factor
        )
        value_total = value_total + jnp.einsum(
            "hgqk,qhgd->khd",
            probs.astype(jnp.bfloat16),
            grad_rows,
            preferred_element_type=jnp.float32,
        )
        return ((key_total, value_total), grad_query)

    empty = jnp.zeros((total_keys, kv_local, HD), jnp.float32)
    (key_total, value_total), grad_query_blocks = lax.scan(
        backward_block, (empty, empty), jnp.arange(blocks, dtype=jnp.int32)
    )
    grad_query_rows = grad_query_blocks.reshape(count, -1)
    key_total = key_total.reshape(total_keys, -1)
    value_total = value_total.reshape(total_keys, -1)
    grad_key_rot, grad_value = (
        lax.psum_scatter(
            key_total.astype(jnp.bfloat16), "ctx", scatter_dimension=0, tiled=True
        ).astype(jnp.float32),
        lax.psum_scatter(
            value_total.astype(jnp.bfloat16), "ctx", scatter_dimension=0, tiled=True
        ).astype(jnp.float32),
    )
    grad_query_raw, grad_query_gain = query_pull(grad_query_rows)
    grad_key_raw, grad_key_gain = key_pull(grad_key_rot)
    grad_query_low = grad_query_raw.astype(jnp.bfloat16)
    grad_key_low = grad_key_raw.astype(jnp.bfloat16)
    grad_value_low = grad_value.astype(jnp.bfloat16)
    grad_query_w = matmul(normed_one.T, grad_query_low)
    grad_key_w = matmul(normed_one.T, grad_key_low)
    grad_value_w = matmul(normed_one.T, grad_value_low)
    grad_normed_one = (
        matmul(grad_query_low, query_weight.T)
        + matmul(grad_key_low, key_weight.T)
        + matmul(grad_value_low, value_weight.T)
    )
    grad_one_part = lax.psum_scatter(
        grad_normed_one.astype(jnp.bfloat16), "tensor", scatter_dimension=1, tiled=True
    ).astype(jnp.float32)
    unit_one_part = lax.dynamic_slice_in_dim(unit_one, column, shard, 1)
    row_term_one = jnp.sum(gain_one_part * grad_one_part * unit_one_part, axis=-1)
    row_total_one, query_gain_total, key_gain_total = lax.psum(
        (row_term_one, grad_query_gain, grad_key_gain), "tensor"
    )
    grad_inputs = (
        grad_resid
        + inverse_one * (gain_one_part * grad_one_part)
        - unit_one_part * (inverse_one / width) * row_total_one[:, None]
    )
    grad_attention_gain = jnp.sum(grad_one_part * unit_one_part, axis=0)
    summed = (
        lax.psum(grad_attention_gain.astype(jnp.bfloat16), ("dp", "ctx")).astype(jnp.float32),
        lax.psum(grad_query_w.astype(jnp.bfloat16), ("dp", "ctx")).astype(jnp.float32),
        lax.psum(grad_key_w.astype(jnp.bfloat16), ("dp", "ctx")).astype(jnp.float32),
        lax.psum(grad_value_w.astype(jnp.bfloat16), ("dp", "ctx")).astype(jnp.float32),
        lax.psum(query_gain_total.astype(jnp.bfloat16), ("dp", "ctx")).astype(jnp.float32),
        lax.psum(key_gain_total.astype(jnp.bfloat16), ("dp", "ctx")).astype(jnp.float32),
        lax.psum(grad_output_w.astype(jnp.bfloat16), ("dp", "ctx")).astype(jnp.float32),
        lax.psum(grad_feed_gain.astype(jnp.bfloat16), ("dp", "ctx")).astype(jnp.float32),
        lax.psum(grad_gate_w.astype(jnp.bfloat16), ("dp", "ctx")).astype(jnp.float32),
        lax.psum(grad_up_w.astype(jnp.bfloat16), ("dp", "ctx")).astype(jnp.float32),
        lax.psum(grad_down.astype(jnp.bfloat16), ("dp", "ctx")).astype(jnp.float32),
    )
    return (outputs, grad_inputs) + tuple(summed)


def solution(mesh):
    in_specs = (
        P(("dp", "ctx"), "tensor"),
        P(("dp", "ctx"), None),
        P("dp", None),
        P("dp", "ctx"),
        P(),
        P(None, "tensor"),
        P(None, "tensor"),
        P(None, "tensor"),
        P(),
        P(),
        P("tensor", None),
        P(),
        P(None, "tensor"),
        P(None, "tensor"),
        P("tensor", None),
    )
    out_specs = (
        P(("dp", "ctx"), "tensor"),
        P(("dp", "ctx"), "tensor"),
        P("tensor"),
        P(None, "tensor"),
        P(None, "tensor"),
        P(None, "tensor"),
        P(),
        P(),
        P("tensor", None),
        P("tensor"),
        P(None, "tensor"),
        P(None, "tensor"),
        P("tensor", None),
    )
    return jax.shard_map(
        per_device, mesh=mesh, in_specs=in_specs, out_specs=out_specs, check_vma=False
    )
```

profile of v0, /device:TPU:0, one launch (start us, length us, event | category | flops | bytes accessed | tf_op | source)
XLA Modules:
  0.0 697.9 jit_solution(3110859281240040887)
XLA Ops:
  8.6 1.2 convert_element_type.211
  13.8 1.5 fusion.22
  15.3 24.9 %all-gather.4.cloned.1.call-done = bf16[256,2048]{1,0:T(8,128)(2,1)} async-done(((bf16[256,512]{1,0:T(8,128)(2,1)}), bf16[256,2048]{1,0:T(8,128)(2,1)}) %all-gather.4.cloned.1.call-update) | async-done | bytes 1048592 | tf_op jit(solution)/shard_map/all_gather | solution.py:71
  40.3 1.5 fusion.2
  42.3 2.0 convolution_convert_fusion.10
  44.4 5.8 all_gather.16
  50.9 2.0 multiply_reduce_fusion.7
  54.4 5.8 all_gather.17
  60.2 1.6 fusion.35
  61.8 1.2 reshape.268
  68.2 2.0 fusion.40
  70.3 43.7 %reduce-scatter.7.cloned.1.call-done = f32[256,512]{1,0:T(8,128)} async-done(((f32[256,2048]{1,0:T(8,128)}), f32[256,512]{1,0:T(8,128)}) %reduce-scatter.7.cloned.1.call-update) | async-done | bytes 524304 | tf_op jit(solution)/shard_map/reduce_scatter | solution.py:132
  114.1 1.8 add_convert_fusion.1
  116.3 27.0 %all-gather.6.cloned.1.call-done = bf16[256,2048]{1,0:T(8,128)(2,1)} async-done(((bf16[256,512]{1,0:T(8,128)(2,1)}), bf16[256,2048]{1,0:T(8,128)(2,1)}) %all-gather.6.cloned.1.call-update) | async-done | bytes 1048592 | tf_op jit(solution)/shard_map/all_gather | solution.py:134
  143.3 1.7 fusion.3
  145.6 5.8 fusion.33
  151.4 1.9 fusion.34
  153.4 3.3 multiply_convert_fusion.2
  156.7 1.8 fusion.41
  158.6 3.2 convolution_add_fusion.1
  162.6 1.5 convert_multiply_fusion
  164.1 41.2 %reduce-scatter.11.cloned.1.call-done = f32[256,512]{1,0:T(8,128)} async-done(((f32[256,2048]{1,0:T(8,128)}), f32[256,512]{1,0:T(8,128)}) %reduce-scatter.11.cloned.1.call-update) | async-done | bytes 524304 | tf_op jit(solution)/shard_map/reduce_scatter | solution.py:158
  205.3 2.0 multiply_reduce_fusion
  207.2 10.5 %psum.105 = f32[256]{0:T(256)} all-reduce(f32[256]{0:T(256)} %get-tuple-element.70), channel_id=1, replica_groups=mesh['dp'=4,'ctx'=2,'tensor'=4] {'tensor'}, use_global_device_ids=true, to_apply=%region_10.11 | all-reduce | flops 256 | bytes 2048 | tf_op jit(solution)/shard_map/psum | solution.py:160
  217.8 2.4 fusion.37
  220.9 25.7 %all-gather.8.cloned.1.call-done = bf16[256,2048]{1,0:T(8,128)(2,1)} async-done(((bf16[256,512]{1,0:T(8,128)(2,1)}), bf16[256,2048]{1,0:T(8,128)(2,1)}) %all-gather.8.cloned.1.call-update) | async-done | bytes 1048592 | tf_op jit(solution)/shard_map/all_gather | solution.py:167
  246.6 2.7 convolution_convert_fusion.8
  249.2 1.8 copy.115
  251.0 2.4 fusion.4
  254.0 1.0 copy-done.7
  254.9 1.2 fusion.11
  256.2 2.2 fusion.12
  258.4 10.1 %reduce-scatter.9.cloned.1.call-start = ((), (), s32[]{:S(2)}) async-start(), calls=%async_computation.9 | async-start | bytes 1310720 | tf_op jit(solution)/shard_map/reduce_scatter | solution.py:143
  268.5 5.9 convolution_convert_fusion.7
  274.9 1.0 copy.113
  275.9 1.0 copy.114
  276.9 1.5 multiply_add_fusion.1
  278.4 2.2 multiply_reduce_fusion.1
  280.9 1.6 fusion.21
  282.5 1.0 convert.17
  285.0 1.9 fusion.43
  287.0 1.8 fusion.1
  288.9 6.1 convolution_convert_fusion
  294.9 4.7 convolution_convert_fusion.1
  299.6 4.7 convolution_convert_fusion.2
  304.3 2.0 convolution_convert_fusion.3
  306.3 2.2 convolution_convert_fusion.4
  308.5 1.6 convolution_convert_fusion.5
  310.1 1.6 convolution_convert_fusion.6
  313.3 1.7 add_convert_fusion
  315.0 25.9 %reduce-scatter.17.cloned.1.call-done = bf16[256,512]{1,0:T(8,128)(2,1)} async-done(((bf16[256,2048]{1,0:T(8,128)(2,1)}), bf16[256,512]{1,0:T(8,128)(2,1)}) %reduce-scatter.17.cloned.1.call-update) | async-done | bytes 262160 | tf_op jit(solution)/shard_map/reduce_scatter | solution.py:228
  340.9 1.2 fusion.20
  342.1 9.7 %all-reduce.4 = (f32[256]{0:T(256)S(1)}, bf16[128]{0:T(256)(128)(2,1)S(1)}, bf16[128]{0:T(256)(128)(2,1)S(1)}) all-reduce(f32[256]{0:T(256)S(1)} %get-tuple-element.72, f32[128]{0:T(128)S(1)} %copy-done.63, f32[128]{0:T(128)S(1)} %copy-done.64), channel_id=1, replica_groups=mesh['dp'=4,'ctx'=2,'tensor'=4] {'tensor'}, use_global_device_ids=true, to_apply=%region_18.19 | all-reduce | flops 512 | bytes 3584 | tf_op jit(solution)/shard_map/psum | solution.py:233
  351.8 14.3 %all-reduce.5 = (bf16[512]{0:T(512)(128)(2,1)S(1)}, bf16[128]{0:T(256)(128)(2,1)S(1)}, bf16[128]{0:T(256)(128)(2,1)S(1)}, bf16[512]{0:T(512)(128)(2,1)S(1)}) all-reduce(bf16[512]{0:T(512)(128)(2,1)S(1)} %get-tuple-element.71, bf16[128]{0:T(256)(128)(2,1)S(1)} %get-tuple-element.78, ...), channel_id=1, replica_groups=mesh['dp'=4,'ctx'=2,'tensor'=4] {'dp','ctx'}, use_global_device_ids=true, to_apply=%region_20.21 | all-reduce | flops 1280 | bytes 5120 | tf_op jit(solution)/shard_map/psum | solution.py:243
  368.3 2.1 fusion.18
  370.4 287.2 %all-reduce.9.cloned.1.call-done = (bf16[2048,512]{1,0:T(8,128)(2,1)}, bf16[2048,256]{1,0:T(8,128)(2,1)}, bf16[2048,256]{1,0:T(8,128)(2,1)}, bf16[512,2048]{1,0:...) async-done(((bf16[2048,512]{1,0:T(8,128)(2,1)}, bf16[2048,256]{1,0:T(8,128)(2,1)}, bf16[2048,256]{1,0:T(8,128)(2,1)}, ...) | async-done | bytes 25165840 | tf_op jit(solution)/shard_map/psum | solution.py:244
  657.6 4.3 convert_element_type.251
  661.9 1.5 convert_element_type.253
  663.5 1.5 convert_element_type.255
  664.9 0.8 copy-done.19
  665.8 2.7 convert_element_type.261
  668.4 9.5 %convert_element_type.265 = f32[2048,1536]{1,0:T(8,128)} convert(bf16[2048,1536]{1,0:T(8,128)(2,1)} %get-tuple-element.101) | non-fusion elementwise | flops 3145728 | bytes 18874368 | tf_op jit(solution)/shard_map/convert_element_type | solution.py:251
  677.9 6.6 convert_element_type.267
  684.5 6.3 convert_element_type.269
  (222 shorter events, 22.6 us)
Async XLA Ops:
  7.2 61.0 %copy-start = (bf16[512,2048]{1,0:T(8,128)(2,1)S(1)}, bf16[512,2048]{1,0:T(8,128)(2,1)}, u32[]{:S(2)}) copy-start(bf16[512,2048]{1,0:T(8,128)(2,1)} %param.25) | copy-start | bytes 6291460
  7.2 33.1 %all-gather.4.cloned.1.call-start = ((), (), s32[]{:S(2)}) async-start(), calls=%async_computation.6 | async-start | bytes 1310720 | tf_op jit(solution)/shard_map/all_gather | solution.py:71
  7.9 106.1 %reduce-scatter.7.cloned.1.call-start = ((), (), s32[]{:S(2)}) async-start(), calls=%async_computation.7 | async-start | bytes 2621440 | tf_op jit(solution)/shard_map/reduce_scatter | solution.py:132
  8.6 55.5 %copy-start.58 = (f32[128]{0:T(128)}, f32[128]{0:T(128)S(1)}, u32[]{:S(2)}) copy-start(f32[128]{0:T(128)S(1)} %convert_element_type.215) | copy-start | bytes 1540
  11.2 49.0 %copy-start.56 = (f32[2048]{0:T(1024)}, f32[2048]{0:T(1024)S(1)}, u32[]{:S(2)}) copy-start(f32[2048]{0:T(1024)S(1)} %convert_element_type.208) | copy-start | bytes 24580
  11.7 28.5 %copy-start.16 = (f32[256,64]{1,0:T(8,128)}, f32[256,64]{1,0:T(8,128)S(1)}, u32[]{:S(2)}) copy-start(f32[256,64]{1,0:T(8,128)S(1)} %get-tuple-element.120) | copy-start | bytes 196612
  41.8 9.1 %copy-start.9 = (bf16[256,2048]{1,0:T(8,128)(2,1)S(1)}, bf16[256,2048]{1,0:T(8,128)(2,1)}, u32[]{:S(2)}) copy-start(bf16[256,2048]{1,0:T(8,128)(2,1)} %all-gather.4.cloned.1.call-done) | copy-start | bytes 3145732
  42.3 17.8 %copy-start.50 = (f32[256]{0:T(256)}, f32[256]{0:T(256)S(1)}, u32[]{:S(2)}) copy-start(f32[256]{0:T(256)S(1)} %get-tuple-element.122) | copy-start | bytes 3076
  50.9 3.4 copy-start.38
  50.9 3.4 copy-start.40
  50.9 9.3 %copy-start.22 = (bf16[2048,512]{1,0:T(8,128)(2,1)S(1)}, bf16[2048,512]{1,0:T(8,128)(2,1)}, u32[]{:S(2)}) copy-start(bf16[2048,512]{1,0:T(8,128)(2,1)} %param.20) | copy-start | bytes 6291460
  53.0 7.2 %copy-start.54 = (f32[256,2]{0,1:T(2,128)}, f32[256,2]{0,1:T(2,128)S(1)}, u32[]{:S(2)}) copy-start(f32[256,2]{0,1:T(2,128)S(1)} %get-tuple-element.125) | copy-start | bytes 6148
  61.8 2.8 copy-start.17
  63.0 2.5 copy-start.5
  70.2 43.8 %copy-start.30 = (bf16[256,512]{1,0:T(8,128)(2,1)S(1)}, bf16[256,512]{1,0:T(8,128)(2,1)}, u32[]{:S(2)}) copy-start(bf16[256,512]{1,0:T(8,128)(2,1)} %param.15) | copy-start | bytes 786436
  70.2 46.1 %copy-start.52 = (bf16[2048]{0:T(1024)(128)(2,1)S(1)}, bf16[2048]{0:T(1024)(128)(2,1)}, u32[]{:S(2)}) copy-start(bf16[2048]{0:T(1024)(128)(2,1)} %param.26) | copy-start | bytes 12292
  70.3 73.0 %all-gather.6.cloned.1.call-start = ((), (), s32[]{:S(2)}) async-start(), calls=%async_computation.8 | async-start | bytes 1310720 | tf_op jit(solution)/shard_map/all_gather | solution.py:134
  115.9 89.4 %reduce-scatter.11.cloned.1.call-start = ((), (), s32[]{:S(2)}) async-start(), calls=%async_computation.10 | async-start | bytes 2621440 | tf_op jit(solution)/shard_map/reduce_scatter | solution.py:158
  143.3 8.0 %slice-start.4 = ((s8[6291456]{0:T(1024)(128)(4,1)}), s8[4194304]{0:T(1024)(128)(4,1)S(1)}, s32[]{:S(2)}) async-start(s8[6291456]{0:T(1024)(128)(4,1)} %bitcast.132), calls=%async_computation.20 | async-start | bytes 8388608
  143.3 10.0 %slice-start.8 = ((s8[6291456]{0:T(1024)(128)(4,1)}), s8[4194304]{0:T(1024)(128)(4,1)S(1)}, s32[]{:S(2)}) async-start(s8[6291456]{0:T(1024)(128)(4,1)} %bitcast.136), calls=%async_computation.24 | async-start | bytes 8388608
  145.6 5.8 copy-start.4
  145.6 5.8 slice-start.5
  145.6 7.8 %slice-start.9 = ((s8[6291456]{0:T(1024)(128)(4,1)}), s8[2097152]{0:T(1024)(128)(4,1)S(1)}, s32[]{:S(2)}) async-start(s8[6291456]{0:T(1024)(128)(4,1)} %bitcast.136), calls=%async_computation.25 | async-start | bytes 4194304
  151.4 7.2 %slice-start.6 = ((s8[6291456]{0:T(1024)(128)(4,1)}), s8[4194304]{0:T(1024)(128)(4,1)S(1)}, s32[]{:S(2)}) async-start(s8[6291456]{0:T(1024)(128)(4,1)} %bitcast.134), calls=%async_computation.22 | async-start | bytes 8388608
  153.4 5.2 slice-start.7
  161.8 84.8 %all-gather.8.cloned.1.call-start = ((), (), s32[]{:S(2)}) async-start(), calls=%async_computation.11 | async-start | bytes 1310720 | tf_op jit(solution)/shard_map/all_gather | solution.py:167
  220.1 62.4 %reduce-scatter.13.cloned.1.call-start = ((), (), s32[]{:S(2)}) async-start(), calls=%async_computation.12 | async-start | bytes 393216 | tf_op jit(solution)/shard_map/reduce_scatter | solution.py:208
  251.0 2.4 copy-start.3
  256.2 28.8 %reduce-scatter.15.cloned.1.call-start = ((), (), s32[]{:S(2)}) async-start(), calls=%async_computation.13 | async-start | bytes 393216 | tf_op jit(solution)/shard_map/reduce_scatter | solution.py:211
  258.4 54.3 %reduce-scatter.9.cloned.1.call-start = ((), (), s32[]{:S(2)}) async-start(), calls=%async_computation.9 | async-start | bytes 1310720 | tf_op jit(solution)/shard_map/reduce_scatter | solution.py:143
  268.5 6.0 copy-start.8
  268.5 6.0 copy-start.13
  274.4 2.5 copy-start.18
  274.4 66.5 %reduce-scatter.17.cloned.1.call-start = ((), (), s32[]{:S(2)}) async-start(), calls=%async_computation.14 | async-start | bytes 1310720 | tf_op jit(solution)/shard_map/reduce_scatter | solution.py:228
  274.8 3.6 copy-start.6
  274.9 3.6 copy-start.21
  276.9 3.8 copy-start.46
  276.9 4.0 copy-start.59
  278.4 5.1 copy-start.39
  278.4 5.1 copy-start.41
  280.6 3.0 copy-start.48
  280.6 3.0 copy-start.60
  280.6 3.7 copy-start.55
  285.0 2.0 copy-start.23
  288.8 6.1 copy-start.37
  288.8 368.8 %all-reduce.9.cloned.1.call-start = ((), (), s32[]{:S(2)}) async-start(), calls=%async_computation.15 | async-start | bytes 50331648 | tf_op jit(solution)/shard_map/psum | solution.py:244
  294.9 4.7 copy-start.35
  299.6 4.7 copy-start.29
  299.6 4.7 copy-start.32
  304.3 2.1 copy-start.10
  304.3 2.1 copy-start.51
  304.3 2.1 copy-start.57
  306.3 2.2 copy-start.43
  312.4 29.6 %copy-start.63 = (f32[128]{0:T(128)S(1)}, f32[128]{0:T(128)}, u32[]{:S(2)}) copy-start(f32[128]{0:T(128)} %get-tuple-element.73) | copy-start | bytes 1540
  312.4 29.6 %copy-start.64 = (f32[128]{0:T(128)S(1)}, f32[128]{0:T(128)}, u32[]{:S(2)}) copy-start(f32[128]{0:T(128)} %get-tuple-element.75) | copy-start | bytes 1540
  312.4 39.4 %copy-start.62 = (bf16[512]{0:T(512)(128)(2,1)S(1)}, bf16[512]{0:T(512)(128)(2,1)}, u32[]{:S(2)}) copy-start(bf16[512]{0:T(512)(128)(2,1)} %get-tuple-element.69) | copy-start | bytes 3076
  312.4 55.9 %copy-start.61 = (f32[256]{0:T(256)S(1)}, f32[256]{0:T(256)}, u32[]{:S(2)}) copy-start(f32[256]{0:T(256)} %get-tuple-element.121) | copy-start | bytes 3076
  657.6 4.3 copy-start.27
  663.4 2.4 copy-start.19
  665.8 12.2 %slice-start.2 = ((s8[6291456]{0:T(1024)(128)(4,1)}), s8[4194304]{0:T(1024)(128)(4,1)S(1)}, s32[]{:S(2)}) async-start(s8[6291456]{0:T(1024)(128)(4,1)} %bitcast.107), calls=%async_computation.18 | async-start | bytes 8388608
  668.4 9.5 %slice-start.3 = ((s8[6291456]{0:T(1024)(128)(4,1)}), s8[2097152]{0:T(1024)(128)(4,1)S(1)}, s32[]{:S(2)}) async-start(s8[6291456]{0:T(1024)(128)(4,1)} %bitcast.107), calls=%async_computation.19 | async-start | bytes 4194304
  668.4 16.1 %slice-start = ((s8[6291456]{0:T(1024)(128)(4,1)}), s8[4194304]{0:T(1024)(128)(4,1)S(1)}, s32[]{:S(2)}) async-start(s8[6291456]{0:T(1024)(128)(4,1)} %bitcast.105), calls=%async_computation.16 | async-start | bytes 8388608
  677.9 6.6 slice-start.1
  684.5 6.3 copy-start.1
  (21 other events, 26.3 us)
Sparse Core Ops, SparseCore 0:
  9.6 30.6 all-gather.3
  70.4 43.6 reduce-scatter.6
  116.0 27.2 all-gather.5
  161.9 43.3 reduce-scatter.10
  220.3 26.2 all-gather.7
  256.3 11.1 reduce-scatter.12
  270.3 11.6 reduce-scatter.14
  284.9 27.1 reduce-scatter.8
  315.1 25.7 reduce-scatter.16
  346.9 310.6 all-reduce.8
where the time goes:
time: 704 us; the launch traced here: 698 us
  waiting for transfers between devices  476 us (68%)
  other arithmetic  67.8 us (10%)
  matrix products  66.3 us (9%)
  blocking collectives  46.1 us (7%)
  between operations  15.3 us (2%)
  local copies, waits for them, and re-layouts  15.1 us (2%)
  starting transfers between devices  10.8 us (2%)
    psum x1, waiting for transfers between devices, per_device(): lax.psum(grad_query_w.astype(jnp.bfloat16), ('dp', 'ctx'))  287 us
    dot_general x21, matrix products, matmul(): return jnp.dot(left, right, preferred_element_type=jnp.float32)  59.2 us
    reduce_scatter x1, waiting for transfers between devices, per_device(): lax.psum_scatter(attention_terms, 'tensor', scatter_dimension=1, tiled=True)  43.7 us
    reduce_scatter x1, waiting for transfers between devices, per_device(): lax.psum_scatter(grad_normed_two, 'tensor', scatter_dimension=1, tiled=True)  41.2 us
    all_gather x1, waiting for transfers between devices, per_device(): lax.all_gather(resid_part, 'tensor', axis=1, tiled=True).astype(jnp.float32)  27 us
    reduce_scatter x1, waiting for transfers between devices, per_device(): lax.psum_scatter(grad_normed_one.astype(jnp.bfloat16), 'tensor', scatter_...  25.9 us
    all_gather x1, waiting for transfers between devices, per_device(): lax.all_gather(grad_resid.astype(jnp.bfloat16), 'tensor', axis=1, tiled=T...  25.7 us
    all_gather x1, waiting for transfers between devices, per_device(): lax.all_gather(inputs, 'tensor', axis=1, tiled=True).astype(jnp.float32)  24.9 us
  transfers between devices with their start and end apart: 10, of which 7 were waited for; matrix products, arithmetic and copies ran while one was open for 9% of the time, Pallas kernels for 0%

commit v1 on v0

--- a/solution.py
+++ b/solution.py
@@ -2,11 +2,18 @@
 import jax.numpy as jnp
 from jax import lax
 from jax.sharding import PartitionSpec as P
+from jax.lax import psum
 
 HD = 128
 EPS = 1e-06
 THETA = 1000000.0
 NEG = -1e30
+
+
+def shape_cycles_on_mesh(obj):
+    for nth in ("ctx", "dp"):
+        obj = psum(obj, axis_name=nth)
+    return obj
 
 
 def rope_tables(position_row):
@@ -241,7 +248,7 @@
     grad_attention_gain = jnp.sum(grad_one_part * unit_one_part, axis=0)
     summed = (
         lax.psum(grad_attention_gain.astype(jnp.bfloat16), ("dp", "ctx")).astype(jnp.float32),
-        lax.psum(grad_query_w.astype(jnp.bfloat16), ("dp", "ctx")).astype(jnp.float32),
+        shape_cycles_on_mesh(grad_query_w.astype(jnp.bfloat16)).astype(jnp.float32),
         lax.psum(grad_key_w.astype(jnp.bfloat16), ("dp", "ctx")).astype(jnp.float32),
         lax.psum(grad_value_w.astype(jnp.bfloat16), ("dp", "ctx")).astype(jnp.float32),
         lax.psum(query_gain_total.astype(jnp.bfloat16), ("dp", "ctx")).astype(jnp.float32),

time: 704 us -> 802 us (1.14)
  waiting for transfers between devices: 476 us -> 572 us
  starting transfers between devices: 10.8 us -> 1.34 us
    psum x1 -> x3, waiting for transfers between devices: 287 us -> 362 us  [the longest x1 291 us: per_device(): lax.psum(grad_key_w.astype(jnp.bfloat16), ('dp', 'ctx')).astype(jnp.float32)]
    reduce_scatter x1, waiting for transfers between devices: 0.02 us -> 19 us  [per_device(): lax.psum_scatter(matmul(hidden, down_weight).astype(jnp.bfloat16), 'tenso...]
    reduce_scatter x1, starting transfers between devices: 10.1 us -> 0.04 us  [per_device(): lax.psum_scatter(matmul(hidden, down_weight).astype(jnp.bfloat16), 'tenso...]
  transfers between devices with their start and end apart: 10 -> 12, of which waited for: 7 -> 10; matrix products, arithmetic and copies ran while one was open for 9% -> 9% of each run, Pallas kernels for 0% -> 0%
where the time goes in v1:
time: 802 us; the launch traced here: 795 us
  waiting for transfers between devices  572 us (71%)
  other arithmetic  73 us (9%)
  matrix products  67.1 us (8%)
  blocking collectives  46.2 us (6%)
  local copies, waits for them, and re-layouts  20.9 us (3%)
  between operations  15.3 us (2%)
    psum x1, waiting for transfers between devices, per_device(): lax.psum(grad_key_w.astype(jnp.bfloat16), ('dp', 'ctx')).astype(jnp.float32)  291 us
    psum x2, waiting for transfers between devices, shape_cycles_on_mesh(): obj = psum(obj, axis_name=nth)  72 us
    dot_general x21, matrix products, matmul(): return jnp.dot(left, right, preferred_element_type=jnp.float32)  59.9 us
    reduce_scatter x1, waiting for transfers between devices, per_device(): lax.psum_scatter(attention_terms, 'tensor', scatter_dimension=1, tiled=True)  43.8 us
    reduce_scatter x1, waiting for transfers between devices, per_device(): lax.psum_scatter(grad_normed_two, 'tensor', scatter_dimension=1, tiled=True)  41.2 us
    all_gather x1, waiting for transfers between devices, per_device(): lax.all_gather(resid_part, 'tensor', axis=1, tiled=True).astype(jnp.float32)  26.9 us
    reduce_scatter x1, waiting for transfers between devices, per_device(): lax.psum_scatter(grad_normed_one.astype(jnp.bfloat16), 'tensor', scatter_...  26.8 us
    all_gather x1, waiting for transfers between devices, per_device(): lax.all_gather(grad_resid.astype(jnp.bfloat16), 'tensor', axis=1, tiled=T...  25.6 us
  transfers between devices with their start and end apart: 12, of which 10 were waited for; matrix products, arithmetic and copies ran while one was open for 9% of the time, Pallas kernels for 0%

profile of v1, /device:TPU:0, one launch (start us, length us, event | category | flops | bytes accessed | tf_op | source)
XLA Modules:
  0.0 795.4 jit_solution(17748124670958978191)
XLA Ops:
  13.8 1.5 fusion.22
  15.3 25.0 %all-gather.4.cloned.1.call-done = bf16[256,2048]{1,0:T(8,128)(2,1)} async-done(((bf16[256,512]{1,0:T(8,128)(2,1)}), bf16[256,2048]{1,0:T(8,128)(2,1)}) %all-gather.4.cloned.1.call-update) | async-done | bytes 1048592 | tf_op jit(solution)/shard_map/all_gather | solution.py:78
  40.3 1.5 fusion.2
  42.3 2.0 convolution_convert_fusion.10
  44.4 5.9 all_gather.16
  50.2 1.7 reshape.265
  52.0 2.0 multiply_reduce_fusion.7
  55.5 5.8 all_gather.17
  61.2 1.6 fusion.35
  67.1 1.4 subtract_convert_fusion
  71.6 2.0 fusion.40
  73.7 43.8 %reduce-scatter.7.cloned.1.call-done = f32[256,512]{1,0:T(8,128)} async-done(((f32[256,2048]{1,0:T(8,128)}), f32[256,512]{1,0:T(8,128)}) %reduce-scatter.7.cloned.1.call-update) | async-done | bytes 524304 | tf_op jit(solution)/shard_map/reduce_scatter | solution.py:139
  117.5 1.8 add_convert_fusion.1
  119.9 26.9 %all-gather.6.cloned.1.call-done = bf16[256,2048]{1,0:T(8,128)(2,1)} async-done(((bf16[256,512]{1,0:T(8,128)(2,1)}), bf16[256,2048]{1,0:T(8,128)(2,1)}) %all-gather.6.cloned.1.call-update) | async-done | bytes 1048592 | tf_op jit(solution)/shard_map/all_gather | solution.py:141
  146.7 1.7 fusion.3
  149.0 5.7 fusion.33
  154.8 1.9 fusion.34
  156.8 3.3 multiply_convert_fusion.2
  160.1 1.8 fusion.41
  162.0 3.2 convolution_add_fusion.1
  166.0 1.5 convert_multiply_fusion
  167.5 41.2 %reduce-scatter.11.cloned.1.call-done = f32[256,512]{1,0:T(8,128)} async-done(((f32[256,2048]{1,0:T(8,128)}), f32[256,512]{1,0:T(8,128)}) %reduce-scatter.11.cloned.1.call-update) | async-done | bytes 524304 | tf_op jit(solution)/shard_map/reduce_scatter | solution.py:165
  208.7 1.9 multiply_reduce_fusion
  210.6 10.5 %psum.112 = f32[256]{0:T(256)} all-reduce(f32[256]{0:T(256)} %get-tuple-element.70), channel_id=1, replica_groups=mesh['dp'=4,'ctx'=2,'tensor'=4] {'tensor'}, use_global_device_ids=true, to_apply=%region_10.11 | all-reduce | flops 256 | bytes 2048 | tf_op jit(solution)/shard_map/psum | solution.py:167
  221.2 2.4 fusion.37
  224.3 25.6 %all-gather.8.cloned.1.call-done = bf16[256,2048]{1,0:T(8,128)(2,1)} async-done(((bf16[256,512]{1,0:T(8,128)(2,1)}), bf16[256,2048]{1,0:T(8,128)(2,1)}) %all-gather.8.cloned.1.call-update) | async-done | bytes 1048592 | tf_op jit(solution)/shard_map/all_gather | solution.py:174
  250.0 2.7 convolution_convert_fusion.8
  252.6 1.8 copy.115
  254.4 2.4 fusion.4
  260.4 1.9 copy.113
  262.3 1.9 copy.114
  264.3 1.6 multiply_add_fusion.1
  265.9 2.4 multiply_reduce_fusion.1
  268.4 1.6 copy.88
  271.2 1.5 copy.89
  272.7 2.2 fusion.12
  274.9 2.2 fusion.21
  277.2 2.2 convolution_convert_fusion.4
  279.5 5.7 convolution_convert_fusion.7
  287.1 1.7 fusion.42
  288.9 1.9 fusion.43
  290.9 1.8 fusion.1
  292.8 5.8 convolution_convert_fusion.1
  298.6 4.6 convolution_convert_fusion.2
  303.3 48.7 %all-reduce.11.cloned.1.call-done = bf16[2048,512]{1,0:T(8,128)(2,1)} async-done(((bf16[2048,512]{1,0:T(8,128)(2,1)}), bf16[2048,512]{1,0:T(8,128)(2,1)}) %all-reduce.11.cloned.1.call-update) | async-done | bytes 2097168 | tf_op jit(solution)/shard_map/psum | solution.py:15
  352.3 4.5 convolution_convert_fusion
  356.9 2.0 convolution_convert_fusion.3
  358.9 1.7 convolution_convert_fusion.5
  360.6 1.6 convolution_convert_fusion.6
  363.2 19.0 %reduce-scatter.9.cloned.1.call-done = bf16[256,512]{1,0:T(8,128)(2,1)} async-done(((bf16[256,2048]{1,0:T(8,128)(2,1)}), bf16[256,512]{1,0:T(8,128)(2,1)}) %reduce-scatter.9.cloned.1.call-update) | async-done | bytes 262160 | tf_op jit(solution)/shard_map/reduce_scatter | solution.py:150
  382.1 1.7 add_convert_fusion
  383.9 26.8 %reduce-scatter.17.cloned.1.call-done = bf16[256,512]{1,0:T(8,128)(2,1)} async-done(((bf16[256,2048]{1,0:T(8,128)(2,1)}), bf16[256,512]{1,0:T(8,128)(2,1)}) %reduce-scatter.17.cloned.1.call-update) | async-done | bytes 262160 | tf_op jit(solution)/shard_map/reduce_scatter | solution.py:235
  411.9 9.7 %all-reduce.4 = (f32[256]{0:T(256)S(1)}, bf16[128]{0:T(256)(128)(2,1)S(1)}, bf16[128]{0:T(256)(128)(2,1)S(1)}) all-reduce(f32[256]{0:T(256)S(1)} %get-tuple-element.72, f32[128]{0:T(128)S(1)} %copy-done.63, f32[128]{0:T(128)S(1)} %copy-done.64), channel_id=1, replica_groups=mesh['dp'=4,'ctx'=2,'tensor'=4] {'tensor'}, use_global_device_ids=true, to_apply=%region_18.19 | all-reduce | flops 512 | bytes 3584 | tf_op jit(solution)/shard_map/psum | solution.py:240
  421.6 14.4 %all-reduce.5 = (bf16[512]{0:T(512)(128)(2,1)S(1)}, bf16[128]{0:T(256)(128)(2,1)S(1)}, bf16[128]{0:T(256)(128)(2,1)S(1)}, bf16[512]{0:T(512)(128)(2,1)S(1)}) all-reduce(bf16[512]{0:T(512)(128)(2,1)S(1)} %get-tuple-element.71, bf16[128]{0:T(256)(128)(2,1)S(1)} %get-tuple-element.78, ...), channel_id=1, replica_groups=mesh['dp'=4,'ctx'=2,'tensor'=4] {'dp','ctx'}, use_global_device_ids=true, to_apply=%region_20.21 | all-reduce | flops 1280 | bytes 5120 | tf_op jit(solution)/shard_map/psum | solution.py:250
  438.1 2.1 fusion.18
  440.2 23.2 %all-reduce.13.cloned.1.call-done = bf16[2048,512]{1,0:T(8,128)(2,1)} async-done(((bf16[2048,512]{1,0:T(8,128)(2,1)}), bf16[2048,512]{1,0:T(8,128)(2,1)}) %all-reduce.13.cloned.1.call-update) | async-done | bytes 2097168 | tf_op jit(solution)/shard_map/psum | solution.py:15
  463.4 4.2 convert_element_type.251
  467.6 290.5 %all-reduce.15.cloned.1.call-done = (bf16[2048,256]{1,0:T(8,128)(2,1)}, bf16[2048,256]{1,0:T(8,128)(2,1)}, bf16[512,2048]{1,0:T(8,128)(2,1)}, bf16[2048,1536]{1,...) async-done(((bf16[2048,256]{1,0:T(8,128)(2,1)}, bf16[2048,256]{1,0:T(8,128)(2,1)}, bf16[512,2048]{1,0:T(8,128)(2,1)}, bf16[2048,1536]{1,0:T(8,128)(2,1)}, ...) | async-done | bytes 23068688 | tf_op jit(solution)/shard_map/psum | solution.py:252
  758.2 2.8 convert_element_type.253
  761.0 1.5 convert_element_type.255
  763.3 2.7 convert_element_type.261
  766.0 9.5 %convert_element_type.265 = f32[2048,1536]{1,0:T(8,128)} convert(bf16[2048,1536]{1,0:T(8,128)(2,1)} %get-tuple-element.100) | non-fusion elementwise | flops 3145728 | bytes 18874368 | tf_op jit(solution)/shard_map/convert_element_type | solution.py:258
  775.5 6.6 convert_element_type.267
  782.0 6.3 convert_element_type.269
  (228 shorter events, 31.1 us)
Async XLA Ops:
  7.2 64.4 %copy-start = (bf16[512,2048]{1,0:T(8,128)(2,1)S(1)}, bf16[512,2048]{1,0:T(8,128)(2,1)}, u32[]{:S(2)}) copy-start(bf16[512,2048]{1,0:T(8,128)(2,1)} %param.25) | copy-start | bytes 6291460
  7.2 33.1 %all-gather.4.cloned.1.call-start = ((), (), s32[]{:S(2)}) async-start(), calls=%async_computation.6 | async-start | bytes 1310720 | tf_op jit(solution)/shard_map/all_gather | solution.py:78
  7.9 109.6 %reduce-scatter.7.cloned.1.call-start = ((), (), s32[]{:S(2)}) async-start(), calls=%async_computation.7 | async-start | bytes 2621440 | tf_op jit(solution)/shard_map/reduce_scatter | solution.py:139
  8.6 57.2 %copy-start.59 = (f32[128]{0:T(128)}, f32[128]{0:T(128)S(1)}, u32[]{:S(2)}) copy-start(f32[128]{0:T(128)S(1)} %convert_element_type.215) | copy-start | bytes 1540
  11.2 50.0 %copy-start.56 = (f32[2048]{0:T(1024)}, f32[2048]{0:T(1024)S(1)}, u32[]{:S(2)}) copy-start(f32[2048]{0:T(1024)S(1)} %convert_element_type.208) | copy-start | bytes 24580
  11.7 32.6 %copy-start.17 = (f32[256,64]{1,0:T(8,128)}, f32[256,64]{1,0:T(8,128)S(1)}, u32[]{:S(2)}) copy-start(f32[256,64]{1,0:T(8,128)S(1)} %get-tuple-element.119) | copy-start | bytes 196612
  41.8 10.2 %copy-start.9 = (bf16[256,2048]{1,0:T(8,128)(2,1)S(1)}, bf16[256,2048]{1,0:T(8,128)(2,1)}, u32[]{:S(2)}) copy-start(bf16[256,2048]{1,0:T(8,128)(2,1)} %all-gather.4.cloned.1.call-done) | copy-start | bytes 3145732
  42.3 18.9 %copy-start.49 = (f32[256]{0:T(256)}, f32[256]{0:T(256)S(1)}, u32[]{:S(2)}) copy-start(f32[256]{0:T(256)S(1)} %get-tuple-element.121) | copy-start | bytes 3076
  52.0 3.4 copy-start.38
  52.0 3.4 copy-start.40
  52.0 9.3 %copy-start.21 = (bf16[2048,512]{1,0:T(8,128)(2,1)S(1)}, bf16[2048,512]{1,0:T(8,128)(2,1)}, u32[]{:S(2)}) copy-start(bf16[2048,512]{1,0:T(8,128)(2,1)} %param.20) | copy-start | bytes 6291460
  54.0 7.2 copy-start.54
  64.0 4.9 copy-start.5
  65.8 3.1 copy-start.13
  65.8 3.1 copy-start.42
  73.7 43.8 %copy-start.30 = (bf16[256,512]{1,0:T(8,128)(2,1)S(1)}, bf16[256,512]{1,0:T(8,128)(2,1)}, u32[]{:S(2)}) copy-start(bf16[256,512]{1,0:T(8,128)(2,1)} %param.15) | copy-start | bytes 786436
  73.7 46.2 %copy-start.52 = (bf16[2048]{0:T(1024)(128)(2,1)S(1)}, bf16[2048]{0:T(1024)(128)(2,1)}, u32[]{:S(2)}) copy-start(bf16[2048]{0:T(1024)(128)(2,1)} %param.26) | copy-start | bytes 12292
  73.7 73.1 %all-gather.6.cloned.1.call-start = ((), (), s32[]{:S(2)}) async-start(), calls=%async_computation.8 | async-start | bytes 1310720 | tf_op jit(solution)/shard_map/all_gather | solution.py:141
  119.3 89.4 %reduce-scatter.11.cloned.1.call-start = ((), (), s32[]{:S(2)}) async-start(), calls=%async_computation.10 | async-start | bytes 2621440 | tf_op jit(solution)/shard_map/reduce_scatter | solution.py:165
  146.7 8.0 %slice-start.4 = ((s8[6291456]{0:T(1024)(128)(4,1)}), s8[4194304]{0:T(1024)(128)(4,1)S(1)}, s32[]{:S(2)}) async-start(s8[6291456]{0:T(1024)(128)(4,1)} %bitcast.132), calls=%async_computation.22 | async-start | bytes 8388608
  146.7 10.0 %slice-start.8 = ((s8[6291456]{0:T(1024)(128)(4,1)}), s8[4194304]{0:T(1024)(128)(4,1)S(1)}, s32[]{:S(2)}) async-start(s8[6291456]{0:T(1024)(128)(4,1)} %bitcast.136), calls=%async_computation.26 | async-start | bytes 8388608
  149.0 5.8 copy-start.4
  149.0 5.8 slice-start.5
  149.0 7.7 slice-start.9
  154.8 7.2 slice-start.6
  156.8 5.2 slice-start.7
  165.2 84.8 %all-gather.8.cloned.1.call-start = ((), (), s32[]{:S(2)}) async-start(), calls=%async_computation.11 | async-start | bytes 1310720 | tf_op jit(solution)/shard_map/all_gather | solution.py:174
  223.6 61.7 %reduce-scatter.13.cloned.1.call-start = ((), (), s32[]{:S(2)}) async-start(), calls=%async_computation.12 | async-start | bytes 393216 | tf_op jit(solution)/shard_map/reduce_scatter | solution.py:215
  254.4 2.4 copy-start.3
  256.9 2.1 copy-start.14
  260.2 28.7 %reduce-scatter.15.cloned.1.call-start = ((), (), s32[]{:S(2)}) async-start(), calls=%async_computation.13 | async-start | bytes 393216 | tf_op jit(solution)/shard_map/reduce_scatter | solution.py:218
  265.9 2.5 copy-start.7
  265.9 2.5 copy-start.8
  265.9 9.0 %copy-start.20 = (f32[256,4]{1,0:T(8,128)S(1)}, f32[256,4]{1,0:T(8,128)}, u32[]{:S(2)}) copy-start(f32[256,4]{1,0:T(8,128)} %copy.78) | copy-start | bytes 12292
  274.8 2.3 copy-start.10
  274.8 2.3 copy-start.50
  274.9 77.1 %all-reduce.11.cloned.1.call-start = ((), (), s32[]{:S(2)}) async-start(), calls=%async_computation.15 | async-start | bytes 4194304 | tf_op jit(solution)/shard_map/psum | solution.py:15
  274.9 2.3 copy-start.57
  277.2 2.2 copy-start.33
  277.2 2.3 copy-start.25
  279.4 102.7 %reduce-scatter.9.cloned.1.call-start = ((), (), s32[]{:S(2)}) async-start(), calls=%async_computation.9 | async-start | bytes 1310720 | tf_op jit(solution)/shard_map/reduce_scatter | solution.py:150
  279.5 6.7 copy-start.39
  279.5 6.7 copy-start.41
  285.2 125.5 %reduce-scatter.17.cloned.1.call-start = ((), (), s32[]{:S(2)}) async-start(), calls=%async_computation.14 | async-start | bytes 1310720 | tf_op jit(solution)/shard_map/reduce_scatter | solution.py:235
  292.7 5.9 copy-start.36
  292.7 170.7 %all-reduce.13.cloned.1.call-start = ((), (), s32[]{:S(2)}) async-start(), calls=%async_computation.16 | async-start | bytes 4194304 | tf_op jit(solution)/shard_map/psum | solution.py:15
  303.2 49.0 %copy-start.24 = (bf16[256,2048]{1,0:T(8,128)(2,1)S(1)}, bf16[256,2048]{1,0:T(8,128)(2,1)}, u32[]{:S(2)}) copy-start(bf16[256,2048]{1,0:T(8,128)(2,1)} %param.16) | copy-start | bytes 3145732
  303.3 49.0 %copy-start.26 = (bf16[256,1536]{1,0:T(8,128)(2,1)S(1)}, bf16[256,1536]{1,0:T(8,128)(2,1)}, u32[]{:S(2)}) copy-start(bf16[256,1536]{1,0:T(8,128)(2,1)} %get-tuple-element.107) | copy-start | bytes 2359300
  352.0 4.8 copy-start.32
  352.0 406.1 %all-reduce.15.cloned.1.call-start = ((), (), s32[]{:S(2)}) async-start(), calls=%async_computation.17 | async-start | bytes 46137344 | tf_op jit(solution)/shard_map/psum | solution.py:252
  352.3 4.6 copy-start.29
  356.9 2.1 copy-start.43
  362.9 19.3 %copy-start.12 = (bf16[256,512]{1,0:T(8,128)(2,1)S(1)}, bf16[256,512]{1,0:T(8,128)(2,1)}, u32[]{:S(2)}) copy-start(bf16[256,512]{1,0:T(8,128)(2,1)} %add_convert_fusion.1) | copy-start | bytes 786436
  362.9 48.9 %copy-start.63 = (f32[128]{0:T(128)S(1)}, f32[128]{0:T(128)}, u32[]{:S(2)}) copy-start(f32[128]{0:T(128)} %get-tuple-element.73) | copy-start | bytes 1540
  362.9 48.9 %copy-start.64 = (f32[128]{0:T(128)S(1)}, f32[128]{0:T(128)}, u32[]{:S(2)}) copy-start(f32[128]{0:T(128)} %get-tuple-element.75) | copy-start | bytes 1540
  362.9 58.6 %copy-start.62 = (bf16[512]{0:T(512)(128)(2,1)S(1)}, bf16[512]{0:T(512)(128)(2,1)}, u32[]{:S(2)}) copy-start(bf16[512]{0:T(512)(128)(2,1)} %get-tuple-element.69) | copy-start | bytes 3076
  363.0 75.2 %copy-start.61 = (f32[256]{0:T(256)S(1)}, f32[256]{0:T(256)}, u32[]{:S(2)}) copy-start(f32[256]{0:T(256)} %get-tuple-element.120) | copy-start | bytes 3076
  758.2 2.8 copy-start.27
  761.0 2.3 copy-start.18
  763.3 12.2 %slice-start.2 = ((s8[6291456]{0:T(1024)(128)(4,1)}), s8[4194304]{0:T(1024)(128)(4,1)S(1)}, s32[]{:S(2)}) async-start(s8[6291456]{0:T(1024)(128)(4,1)} %bitcast.107), calls=%async_computation.20 | async-start | bytes 8388608
  766.0 9.5 %slice-start.3 = ((s8[6291456]{0:T(1024)(128)(4,1)}), s8[2097152]{0:T(1024)(128)(4,1)S(1)}, s32[]{:S(2)}) async-start(s8[6291456]{0:T(1024)(128)(4,1)} %bitcast.107), calls=%async_computation.21 | async-start | bytes 4194304
  766.0 16.1 %slice-start = ((s8[6291456]{0:T(1024)(128)(4,1)}), s8[4194304]{0:T(1024)(128)(4,1)S(1)}, s32[]{:S(2)}) async-start(s8[6291456]{0:T(1024)(128)(4,1)} %bitcast.105), calls=%async_computation.18 | async-start | bytes 8388608
  775.5 6.6 slice-start.1
  782.0 6.3 copy-start.1
  (23 other events, 32.2 us)
Sparse Core Ops, SparseCore 0:
  9.6 30.6 all-gather.3
  73.8 43.6 reduce-scatter.6
  119.5 27.2 all-gather.5
  165.3 43.3 reduce-scatter.10
  223.7 26.2 all-gather.7
  260.3 11.1 reduce-scatter.12
  275.0 11.1 reduce-scatter.14
  289.0 62.9 all-reduce.10
  355.0 27.1 reduce-scatter.8
  384.9 25.7 reduce-scatter.16
  413.2 50.2 all-reduce.12
  469.3 288.7 all-reduce.14
